TPU v7x, 256 devices: a whole 4x4x8 slice. The times are simulated.
256 devices in a mesh: dp: 32 (over z_hi, y, core), rows: 8 (over z_lo, x).
Axes of the slice: x: 4, y: 4, z: 8 (z_hi: 4, z_lo: 2; z = z_hi * 2 + z_lo), core: 2. Of those that a mesh axis runs over, the one named last changes fastest.
Arguments:
- latent: bfloat16 [32, 320, 16, 128], P('dp', None, 'rows'), may hold values from -14 to 14
- hint_field: bfloat16 [32, 320, 16, 128], P('dp', None, 'rows'), may hold values from -6 to 6
- from_below: bfloat16 [32, 320, 16, 128], P('dp', None, 'rows'), may hold values from -6 to 6
- cotangent: bfloat16 [32, 320, 16, 128], P('dp', None, 'rows'), may hold values from -6 to 6
- timesteps: int32 [32], P('dp'), may hold values from 0 to 999
- time_weight: bfloat16 [320, 1280], replicated, may hold values from -0.3125 to 0.3125
- enc_proj: bfloat16 [1280, 320], replicated, may hold values from -0.4375 to 0.4375
- ctl_proj: bfloat16 [1280, 320], replicated, may hold values from -0.15625 to 0.15625
- dec_proj: bfloat16 [1280, 320], replicated, may hold values from -0.15625 to 0.15625
- enc_conv_one: bfloat16 [320, 3, 3, 320], replicated, may hold values from -0.109375 to 0.109375
- enc_conv_two: bfloat16 [320, 3, 3, 320], replicated, may hold values from -0.109375 to 0.109375
- ctl_conv_one: bfloat16 [320, 3, 3, 320], P('dp'), may hold values from -0.109375 to 0.109375
- ctl_conv_two: bfloat16 [320, 3, 3, 320], P('dp'), may hold values from -0.109375 to 0.109375
- dec_conv_one: bfloat16 [320, 3, 3, 640], P('dp'), may hold values from -0.078125 to 0.078125
- dec_conv_two: bfloat16 [320, 3, 3, 320], P('dp'), may hold values from -0.109375 to 0.109375
- dec_shortcut: bfloat16 [320, 640], P('dp'), may hold values from -0.25 to 0.25
- zero_conv: bfloat16 [320, 320], P('dp'), may hold values from -0.3125 to 0.3125
Outputs:
- ctl_conv_one_grad: float32 [320, 3, 3, 320], P('dp')
- ctl_conv_two_grad: float32 [320, 3, 3, 320], P('dp')
- zero_conv_grad: float32 [320, 320], P('dp')
All inputs are finite; a program needn't handle non-finite values.
Results may differ from a plain program's by a relative error of at most 0.009.
Values may be sent and summed in bfloat16 or wider, within the bound.
A program may use at most 128 MiB of HBM per device.

v0:
```python
import math
import jax
import jax.numpy as jnp
from jax import lax
from jax.sharding import PartitionSpec as P

C = 320
GROUPS = 32
EPSILON = 1e-05
LAYOUT = ("NCHW", "OHWI", "NCHW")


def extended(x, sides, width):
    for axis, dim in sides:
        peers, length = (lax.axis_size(axis), x.shape[dim])
        up = [(i, (i + 1) % peers) for i in range(peers - 1)]
        down = [(j, i) for i, j in up]
        last = lax.slice_in_dim(x, length - width, length, axis=dim)
        first = lax.slice_in_dim(x, 0, width, axis=dim)
        before = lax.ppermute(last, axis, up)
        after = lax.ppermute(first, axis, down)
        x = jnp.concatenate([before, x, after], axis=dim)
    return x


def shifted(value, axis, steps):
    count = lax.axis_size(axis)
    first, last = (max(0, -steps), min(count, count - steps))
    return lax.ppermute(value, axis, [(source, source + steps) for source in range(first, last)])


def conv_rows(padded, weight):
    return lax.conv_general_dilated(
        padded,
        weight,
        (1, 1),
        ((0, 0), (1, 1)),
        dimension_numbers=LAYOUT,
        preferred_element_type=jnp.float32,
    )


def with_halo(source):
    return extended(source, (("rows", 2),), 1)


def mix_channels(matrix, source):
    return jnp.einsum("oi,bihw->bohw", matrix, source, preferred_element_type=jnp.float32)


def mix_back(matrix, upstream):
    return jnp.einsum("oi,bohw->bihw", matrix, upstream, preferred_element_type=jnp.float32)


def flip_kernel(weight):
    return jnp.transpose(weight[:, ::-1, ::-1, :], (3, 1, 2, 0))


def group_norm(source):
    full_shape = source.shape
    grouped = source.reshape(
        full_shape[0], GROUPS, full_shape[1] // GROUPS, full_shape[2], full_shape[3]
    )
    group_count = full_shape[1] // GROUPS * full_shape[2] * full_shape[3] * lax.axis_size("rows")
    group_total, group_square = lax.psum(
        (jnp.sum(grouped, axis=(2, 3, 4)), jnp.sum(grouped * grouped, axis=(2, 3, 4))), "rows"
    )
    average = group_total / group_count
    inv_spread = lax.rsqrt(group_square / group_count - average * average + EPSILON)
    normed = (grouped - average[:, :, None, None, None]) * inv_spread[:, :, None, None, None]
    return (normed.reshape(full_shape), inv_spread)


def norm_back(upstream, normed, inv_spread):
    full_shape = upstream.shape
    groups_here = inv_spread.shape[1]
    grouped = upstream.reshape(
        full_shape[0], groups_here, full_shape[1] // groups_here, full_shape[2], full_shape[3]
    )
    normed_grouped = normed.reshape(grouped.shape)
    group_count = (
        full_shape[1] // groups_here * full_shape[2] * full_shape[3] * lax.axis_size("rows")
    )
    group_total, group_cross = lax.psum(
        (jnp.sum(grouped, axis=(2, 3, 4)), jnp.sum(grouped * normed_grouped, axis=(2, 3, 4))),
        "rows",
    )
    first_mean = (group_total / group_count)[:, :, None, None, None]
    cross_mean = (group_cross / group_count)[:, :, None, None, None]
    result = inv_spread[:, :, None, None, None] * (
        grouped - first_mean - normed_grouped * cross_mean
    )
    return result.reshape(full_shape)


def silu_slope(values):
    sigma = jax.nn.sigmoid(values)
    return sigma * (1.0 + values * (1.0 - sigma))


def input_grad(upstream, weight):
    flipped = flip_kernel(weight)
    padded = jnp.pad(upstream, ((0, 0), (0, 0), (2, 2), (0, 0)))
    spilled = conv_rows(padded, flipped)
    from_next = shifted(spilled[:, :, :1], "rows", -1)
    from_prev = shifted(spilled[:, :, -1:], "rows", 1)
    result = spilled[:, :, 1:-1]
    result = result.at[:, :, :1].add(from_prev)
    result = result.at[:, :, -1:].add(from_next)
    return result


def kernel_grad(upstream, padded):
    wide = jnp.pad(padded, ((0, 0), (0, 0), (0, 0), (1, 1)))
    row_count = upstream.shape[2]
    col_count = upstream.shape[3]
    return jnp.stack(
        [
            jnp.stack(
                [
                    jnp.einsum(
                        "bohw,bihw->oi",
                        upstream,
                        wide[:, :, row_tap : row_tap + row_count, col_tap : col_tap + col_count],
                        preferred_element_type=jnp.float32,
                    )
                    for col_tap in range(3)
                ],
                1,
            )
            for row_tap in range(3)
        ],
        1,
    )


def block_front(source, conv_one, time_term):
    normed_in, spread_in = group_norm(source.astype(jnp.float32))
    first_halo = with_halo(jax.nn.silu(normed_in).astype(jnp.bfloat16))
    inner_sum = conv_rows(first_halo, conv_one) + time_term[:, :, None, None]
    normed, spread = group_norm(inner_sum)
    second_act = jax.nn.silu(normed).astype(jnp.bfloat16)
    return (normed_in, spread_in, first_halo, normed, spread, second_act)


def per_device(
    latent,
    hint_field,
    from_below,
    cotangent,
    timesteps,
    time_weight,
    enc_proj,
    ctl_proj,
    dec_proj,
    enc_conv_one,
    enc_conv_two,
    ctl_conv_one,
    ctl_conv_two,
    dec_conv_one,
    dec_conv_two,
    dec_shortcut,
    zero_conv,
):
    ctl_one, ctl_two, dec_one, dec_two, dec_short, zero_full = (
        lax.all_gather(ctl_conv_one, "dp", axis=0, tiled=True),
        lax.all_gather(ctl_conv_two, "dp", axis=0, tiled=True),
        lax.all_gather(dec_conv_one, "dp", axis=0, tiled=True),
        lax.all_gather(dec_conv_two, "dp", axis=0, tiled=True),
        lax.all_gather(dec_shortcut, "dp", axis=0, tiled=True),
        lax.all_gather(zero_conv, "dp", axis=0, tiled=True),
    )
    half_width = C // 2
    frequency = jnp.exp(-math.log(10000.0) * jnp.arange(half_width, dtype=jnp.float32) / half_width)
    angles = timesteps.astype(jnp.float32)[:, None] * frequency[None, :]
    sinusoid = jnp.concatenate([jnp.cos(angles), jnp.sin(angles)], axis=1).astype(jnp.bfloat16)
    time_embed = jnp.dot(sinusoid, time_weight, preferred_element_type=jnp.float32)
    time_act = jax.nn.silu(time_embed).astype(jnp.bfloat16)
    enc_term = jnp.dot(time_act, enc_proj, preferred_element_type=jnp.float32)
    ctl_term = jnp.dot(time_act, ctl_proj, preferred_element_type=jnp.float32)
    dec_term = jnp.dot(time_act, dec_proj, preferred_element_type=jnp.float32)
    enc_parts = block_front(latent, enc_conv_one, enc_term)
    enc_out = (
        latent.astype(jnp.float32) + conv_rows(with_halo(enc_parts[5]), enc_conv_two)
    ).astype(jnp.bfloat16)
    ctl_in = (latent.astype(jnp.float32) + hint_field.astype(jnp.float32)).astype(jnp.bfloat16)
    ctl_parts = block_front(ctl_in, ctl_one, ctl_term)
    ctl_halo = with_halo(ctl_parts[5])
    ctl_out = (ctl_in.astype(jnp.float32) + conv_rows(ctl_halo, ctl_two)).astype(jnp.bfloat16)
    skip_sum = (enc_out.astype(jnp.float32) + mix_channels(zero_full, ctl_out)).astype(jnp.bfloat16)
    joined = jnp.concatenate([from_below, skip_sum], axis=1)
    dec_parts = block_front(joined, dec_one, dec_term)
    loss_scale = float(
        cotangent.shape[0]
        * lax.axis_size("dp")
        * cotangent.shape[2]
        * lax.axis_size("rows")
        * cotangent.shape[3]
    ) ** (-0.5)
    out_grad = (cotangent.astype(jnp.float32) * loss_scale).astype(jnp.bfloat16)
    dec_second_grad = input_grad(out_grad, dec_two)
    dec_inner_grad = norm_back(
        dec_second_grad * silu_slope(dec_parts[3]), dec_parts[3], dec_parts[4]
    ).astype(jnp.bfloat16)
    skip_first_grad = input_grad(dec_inner_grad, dec_one[:, :, :, C:])
    skip_normed = dec_parts[0][:, C:]
    skip_spread = dec_parts[1][:, GROUPS // 2 :]
    skip_grad = norm_back(
        skip_first_grad * silu_slope(skip_normed), skip_normed, skip_spread
    ) + mix_back(dec_short[:, C:], out_grad)
    skip_grad = skip_grad.astype(jnp.bfloat16)
    zero_local = jnp.einsum("bohw,bihw->oi", skip_grad, ctl_out, preferred_element_type=jnp.float32)
    ctl_out_grad = mix_back(zero_full, skip_grad).astype(jnp.bfloat16)
    two_local = kernel_grad(ctl_out_grad, ctl_halo)
    ctl_second_grad = input_grad(ctl_out_grad, ctl_two)
    ctl_inner_grad = norm_back(
        ctl_second_grad * silu_slope(ctl_parts[3]), ctl_parts[3], ctl_parts[4]
    ).astype(jnp.bfloat16)
    one_local = kernel_grad(ctl_inner_grad, ctl_parts[2])
    owned = (
        lax.psum_scatter(one_local, "dp", scatter_dimension=0, tiled=True),
        lax.psum_scatter(two_local, "dp", scatter_dimension=0, tiled=True),
        lax.psum_scatter(zero_local, "dp", scatter_dimension=0, tiled=True),
    )
    one_grad, two_grad, zero_grad = lax.psum((owned[0], owned[1], owned[2]), "rows")
    return (one_grad, two_grad, zero_grad)


def solution(mesh):
    in_specs = (
        P("dp", None, "rows", None),
        P("dp", None, "rows", None),
        P("dp", None, "rows", None),
        P("dp", None, "rows", None),
        P("dp"),
        P(),
        P(),
        P(),
        P(),
        P(),
        P(),
        P("dp", None, None, None),
        P("dp", None, None, None),
        P("dp", None, None, None),
        P("dp", None, None, None),
        P("dp", None),
        P("dp", None),
    )
    out_specs = (P("dp", None, None, None), P("dp", None, None, None), P("dp", None))
    return jax.shard_map(
        per_device, mesh=mesh, in_specs=in_specs, out_specs=out_specs, check_vma=False
    )
```

profile of v0, /device:TPU:8, one launch (start us, length us, event | category | flops | bytes accessed | tf_op | source)
XLA Modules:
  0.0 869.3 jit_solution(10912018785608878271)
XLA Ops:
  11.7 20.1 %all-reduce.12 = (f32[1,32]{1,0:T(1,128)S(1)}, f32[1,32]{1,0:T(1,128)S(1)}, f32[1,32]{1,0:T(1,128)S(1)}, f32[1,32]{1,0:T(1,128)S(1)}) all-reduce(f32[1,32]{1,0:T(1,128)S(1)} %bitcast.481, f32[1,32]{1,0:T(1,128)S(1)} %bitcast.476, f32[1,32]{1,0:T(1,128)S(1)} %bitcast.479, ...), channel_id=1, replica_groups=mesh['dp'=32,'rows'=8] {'rows'}, use_global_device_ids=true, to_apply=%region_5.6 | all-reduce | flops 128 | bytes 1024 | tf_op jit(solution)/shard_map/psum | solution.py:65
  37.8 5.3 collective-permute-start.2
  44.4 43.7 %all-gather = bf16[32,10,320]{2,1,0:T(8,128)(2,1)S(1)} all-gather(bf16[1,10,320]{2,1,0:T(8,128)(2,1)S(1)} %bitcast.473), channel_id=1, replica_groups=mesh['dp'=32,'rows'=8] {'dp'}, dimensions={0}, use_global_device_ids=true | all-gather | bytes 211200 | tf_op jit(solution)/shard_map/all_gather | solution.py:171
  92.1 2.1 convolution_reduce_fusion.3
  96.3 1.8 fusion.188
  99.2 49.5 %all-gather.1 = bf16[32,10,640]{2,1,0:T(8,128)(2,1)S(1)} all-gather(bf16[1,10,640]{2,1,0:T(8,128)(2,1)S(1)} %bitcast.472), channel_id=1, replica_groups=mesh['dp'=32,'rows'=8] {'dp'}, dimensions={0}, use_global_device_ids=true | all-gather | bytes 422400 | tf_op jit(solution)/shard_map/all_gather | solution.py:170
  149.6 1.5 convolution_reduce_fusion.1
  151.8 1.7 pad_maximum_fusion.2
  155.7 1.7 maximum_bitcast_fusion.8
  159.0 3.1 fusion.27
  162.1 2.0 select_reduce_fusion.3
  165.0 21.3 %all-reduce.11 = (f32[1,32]{1,0:T(1,128)S(1)}, f32[1,32]{1,0:T(1,128)S(1)}, f32[1,32]{1,0:T(1,128)S(1)}, f32[1,32]{1,0:T(1,128)S(1)}) all-reduce(f32[1,32]{1,0:T(1,128)S(1)} %bitcast.480, f32[1,32]{1,0:T(1,128)S(1)} %bitcast.482, f32[1,32]{1,0:T(1,128)S(1)} %bitcast.478, ...), channel_id=1, replica_groups=mesh['dp'=32,'rows'=8] {'rows'}, use_global_device_ids=true, to_apply=%region_8.9 | all-reduce | flops 128 | bytes 1024 | tf_op jit(solution)/shard_map/psum | solution.py:65
  197.6 6.0 collective-permute-start.4
  203.7 3.7 fusion.14
  208.4 4.0 collective-permute-start.10
  217.7 3.1 fusion.20
  222.6 1.6 maximum_bitcast_fusion.7
  229.0 22.0 %all-reduce.10 = (f32[1,32]{1,0:T(1,128)S(1)}, f32[1,32]{1,0:T(1,128)S(1)}) all-reduce(f32[1,32]{1,0:T(1,128)S(1)} %bitcast.484, f32[1,32]{1,0:T(1,128)S(1)} %bitcast.489), channel_id=1, replica_groups=mesh['dp'=32,'rows'=8] {'rows'}, use_global_device_ids=true, to_apply=%region_26.27 | all-reduce | flops 64 | bytes 512 | tf_op jit(solution)/shard_map/psum | solution.py:65
  254.6 1.5 collective-permute-start.9
  256.1 1.8 fusion.131
  257.9 4.0 scatter-add.20
  263.2 2.8 scatter-add.21
  266.0 1.9 maximum_bitcast_fusion.6
  267.9 1.6 copy.299
  269.9 2.9 copy.236
  272.8 2.7 select_reduce_fusion.1
  275.9 21.8 %all-reduce.9 = (f32[1,32]{1,0:T(1,128)S(1)}, f32[1,32]{1,0:T(1,128)S(1)}) all-reduce(f32[1,32]{1,0:T(1,128)S(1)} %bitcast.486, f32[1,32]{1,0:T(1,128)S(1)} %bitcast.490), channel_id=1, replica_groups=mesh['dp'=32,'rows'=8] {'rows'}, use_global_device_ids=true, to_apply=%region_32.33 | all-reduce | flops 64 | bytes 512 | tf_op jit(solution)/shard_map/psum | solution.py:65
  300.5 18.9 %all-reduce.8 = (f32[1,32]{1,0:T(1,128)S(1)}, f32[1,32]{1,0:T(1,128)S(1)}) all-reduce(f32[1,32]{1,0:T(1,128)S(1)} %bitcast.491, f32[1,32]{1,0:T(1,128)S(1)} %bitcast.485), channel_id=1, replica_groups=mesh['dp'=32,'rows'=8] {'rows'}, use_global_device_ids=true, to_apply=%region_41.42 | all-reduce | flops 64 | bytes 512 | tf_op jit(solution)/shard_map/psum | solution.py:84
  320.6 3.5 fusion.17
  326.0 1.9 collective-permute-start.12
  334.6 4.9 collective-permute-done.13
  340.9 20.5 %all-reduce.7 = (f32[1,16]{1,0:T(1,128)S(1)}, f32[1,16]{1,0:T(1,128)S(1)}) all-reduce(f32[1,16]{1,0:T(1,128)S(1)} %bitcast.492, f32[1,16]{1,0:T(1,128)S(1)} %bitcast.487), channel_id=1, replica_groups=mesh['dp'=32,'rows'=8] {'rows'}, use_global_device_ids=true, to_apply=%region_47.48 | all-reduce | flops 32 | bytes 256 | tf_op jit(solution)/shard_map/psum | solution.py:84
  361.7 1.7 fusion.35
  372.2 3.7 fusion.11
  376.3 1.7 collective-permute-start.14
  381.4 5.5 copy.283
  389.9 2.8 scatter-add.26
  392.8 2.4 collective-permute-done.15
  395.5 2.8 scatter-add.29
  399.2 22.1 %all-reduce.6 = (f32[1,32]{1,0:T(1,128)S(1)}, f32[1,32]{1,0:T(1,128)S(1)}) all-reduce(f32[1,32]{1,0:T(1,128)S(1)} %bitcast.488, f32[1,32]{1,0:T(1,128)S(1)} %bitcast.483), channel_id=1, replica_groups=mesh['dp'=32,'rows'=8] {'rows'}, use_global_device_ids=true, to_apply=%region_53.54 | all-reduce | flops 64 | bytes 512 | tf_op jit(solution)/shard_map/psum | solution.py:84
  426.9 5.5 copy.282
  434.3 335.3 %all-reduce.17.cloned.1.call-done = (f32[320,3,3,320]{3,2,1,0:T(4,128)}, f32[320,3,3,320]{3,2,1,0:T(4,128)}, f32[320,320]{1,0:T(8,128)}) async-done(((f32[320,3,3,320]{3,2,1,0:T(4,128)}, f32[320,3,3,320]{3,2,1,0:T(4,128)}, f32[320,320]{1,0:T(8,128)}), (f32[320,3,3,320]{3,2,1,0:T(4,128)}, f32[320,3,3,320]{3,2,1,0:T(4,128)}, f32[320,320]{1,0:T(8,128)})) %all-reduce.17.cloned.1.call-update) | async-done | bytes 7782416
  769.7 1.6 constant_dynamic-slice_fusion.1
  771.3 1.6 constant_dynamic-slice_fusion.2
  773.7 37.2 %psum.167 = f32[10,320]{1,0:T(8,128)} all-reduce(f32[10,320]{1,0:T(8,128)S(1)} %constant_dynamic-slice_fusion), channel_id=1, replica_groups=mesh['dp'=32,'rows'=8] {'rows'}, use_global_device_ids=true, to_apply=%region_59.60 | all-reduce | flops 3200 | bytes 25600 | tf_op jit(solution)/shard_map/psum | solution.py:225
  810.9 48.1 %all-reduce.19.cloned.1.call-done = (f32[10,3,3,320]{3,2,1,0:T(4,128)}, f32[10,3,3,320]{3,2,1,0:T(4,128)}) async-done(((f32[10,3,3,320]{3,2,1,0:T(4,128)}, f32[10,3,3,320]{3,2,1,0:T(4,128)}), (f32[10,3,3,320]{3,2,1,0:T(4,128)}, f32[10,3,3,320]{3,2,1,0:T(4,128)})) %all-reduce.19.cloned.1.call-update) | async-done | bytes 230416 | tf_op jit(solution)/shard_map/psum | solution.py:225
  859.0 1.6 copy.342
  860.6 1.6 copy.343
  (370 shorter events, 91.5 us)
Async XLA Ops:
  7.2 154.9 %copy-start = (bf16[320,3,3,320]{3,0,2,1:T(8,128)(2,1)S(1)}, bf16[320,3,3,320]{3,0,2,1:T(8,128)(2,1)}, u32[]{:S(2)}) copy-start(bf16[320,3,3,320]{3,0,2,1:T(8,128)(2,1)} %param.38) | copy-start | bytes 5529604
  7.2 37.2 %copy-start.34 = (bf16[10,320]{1,0:T(8,128)(2,1)S(1)}, bf16[10,320]{1,0:T(8,128)(2,1)}, u32[]{:S(2)}) copy-start(bf16[10,320]{1,0:T(8,128)(2,1)} %param.45) | copy-start | bytes 19204
  7.2 151.8 %all-gather.7.cloned.1.call-start = ((), (), s32[]{:S(2)}) async-start(), calls=%async_computation | async-start | bytes 3041280 | tf_op jit(solution)/shard_map/all_gather | solution.py:166
  7.9 195.7 %all-gather.13.cloned.1.call-start = ((), (), s32[]{:S(2)}) async-start(), calls=%async_computation.3 | async-start | bytes 3041280 | tf_op jit(solution)/shard_map/all_gather | solution.py:169
  8.7 209.0 %all-gather.9.cloned.1.call-start = ((), (), s32[]{:S(2)}) async-start(), calls=%async_computation.1 | async-start | bytes 3041280 | tf_op jit(solution)/shard_map/all_gather | solution.py:167
  9.4 260.5 %all-gather.11.cloned.1.call-start = ((), (), s32[]{:S(2)}) async-start(), calls=%async_computation.2 | async-start | bytes 5068800 | tf_op jit(solution)/shard_map/all_gather | solution.py:168
  10.7 216.2 %copy-start.3 = (bf16[1,320,2,128]{3,1,2,0:T(8,128)(2,1)}, bf16[1,320,2,128]{3,1,2,0:T(8,128)(2,1)S(1)}, u32[]{:S(2)}) copy-start(bf16[1,320,2,128]{3,1,2,0:T(8,128)(2,1)S(1)} %get-tuple-element.159) | copy-start | bytes 491524
  33.0 118.2 %collective-permute-start = (bf16[1,320,1,128]{3,1,2,0:T(8,128)(2,1)}, bf16[1,320,1,128]{3,1,2,0:T(8,128)(2,1)S(1)}, u32[]{:S(2)}, u32[]{:S(2)}) collective-permute-start(bf16[1,320,1,128]{3,1,2,0:T(8,128)(2,1)} %get-tuple-element.153), channel_id=1, source_target_pairs={{0,1},{1,2},{2,3},{3,4},{4,5},{5,6},{6,7},{8,9},{9,10},{10,11},{11... | collective-permute-start | bytes 245768 | tf_op jit(solution)/shard_map/ppermute | solution.py:20
  34.3 117.5 %collective-permute-start.1 = (bf16[1,320,1,128]{3,1,2,0:T(8,128)(2,1)}, bf16[1,320,1,128]{3,1,2,0:T(8,128)(2,1)}, u32[]{:S(2)}, u32[]{:S(2)}) collective-permute-start(bf16[1,320,1,128]{3,1,2,0:T(8,128)(2,1)} %get-tuple-element.154), channel_id=1, source_target_pairs={{1,0},{2,1},{3,2},{4,3},{5,4},{6,5},{7,6},{9,8},{10,9},{11,10},{12... | collective-permute-start | bytes 245768 | tf_op jit(solution)/shard_map/ppermute | solution.py:21
  37.0 58.6 %copy-start.13 = (bf16[1,320,2,128]{3,1,2,0:T(8,128)(2,1)}, bf16[1,320,2,128]{3,1,2,0:T(8,128)(2,1)S(1)}, u32[]{:S(2)}) copy-start(bf16[1,320,2,128]{3,1,2,0:T(8,128)(2,1)S(1)} %fusion.104) | copy-start | bytes 491524
  37.8 57.9 %copy-start.30 = (bf16[1,320,2,128]{3,2,1,0:T(2,128)(2,1)S(1)}, bf16[1,320,2,128]{3,2,1,0:T(2,128)(2,1)}, u32[]{:S(2)}) copy-start(bf16[1,320,2,128]{3,2,1,0:T(2,128)(2,1)} %param.31) | copy-start | bytes 491524
  37.8 117.3 %collective-permute-start.2 = (bf16[1,320,1,128]{3,1,2,0:T(8,128)(2,1)}, bf16[1,320,1,128]{3,1,2,0:T(8,128)(2,1)}, u32[]{:S(2)}, u32[]{:S(2)}) collective-permute-start(bf16[1,320,1,128]{3,1,2,0:T(8,128)(2,1)} %get-tuple-element.155), channel_id=1, source_target_pairs={{0,1},{1,2},{2,3},{3,4},{4,5},{5,6},{6,7},{8,9},{9,10},{10,11},{11... | collective-permute-start | bytes 245768 | tf_op jit(solution)/shard_map/ppermute | solution.py:20
  43.1 112.0 %collective-permute-start.3 = (bf16[1,320,1,128]{3,1,2,0:T(8,128)(2,1)}, bf16[1,320,1,128]{3,1,2,0:T(8,128)(2,1)}, u32[]{:S(2)}, u32[]{:S(2)}) collective-permute-start(bf16[1,320,1,128]{3,1,2,0:T(8,128)(2,1)} %get-tuple-element.156), channel_id=1, source_target_pairs={{1,0},{2,1},{3,2},{4,3},{5,4},{6,5},{7,6},{9,8},{10,9},{11,10},{12... | collective-permute-start | bytes 245768 | tf_op jit(solution)/shard_map/ppermute | solution.py:21
  44.4 725.3 %all-reduce.17.cloned.1.call-start = ((), (), s32[]{:S(2)}) async-start(), calls=%async_computation.4 | async-start | bytes 24576000
  90.6 8.6 copy-start.31
  149.6 6.1 copy-start.14
  158.9 3.2 copy-start.37
  188.9 5.4 copy-start.21
  190.1 24.9 %collective-permute-start.6 = (bf16[1,320,1,128]{3,1,2,0:T(8,128)(2,1)}, bf16[1,320,1,128]{3,1,2,0:T(8,128)(2,1)S(1)}, u32[]{:S(2)}, u32[]{:S(2)}) collective-permute-start(bf16[1,320,1,128]{3,1,2,0:T(8,128)(2,1)} %bitcast.32), channel_id=1, source_target_pairs={{0,1},{1,2},{2,3},{3,4},{4,5},{5,6},{6,7},{8,9},{9,10},{10,11},{11... | collective-permute-start | bytes 245768 | tf_op jit(solution)/shard_map/ppermute | solution.py:20
  191.5 12.2 %copy-start.29 = (bf16[320,2,1,8,17]{0,3,4,1,2:T(8,128)(2,1)S(1)}, bf16[320,2,1,8,17]{0,3,4,1,2:T(8,128)(2,1)}, u32[]{:S(2)}) copy-start(bf16[320,2,1,8,17]{0,3,4,1,2:T(8,128)(2,1)} %copy-done.28) | copy-start | bytes 522244
  191.5 12.2 %copy-start.38 = (pred[8,17]{0,1:T(8,128)(4,1)S(1)}, pred[8,17]{0,1:T(8,128)(4,1)}, u32[]{:S(2)}) copy-start(pred[8,17]{0,1:T(8,128)(4,1)} %constant.237) | copy-start | bytes 412
  192.3 24.1 %collective-permute-start.7 = (bf16[1,320,1,128]{3,1,2,0:T(8,128)(2,1)}, bf16[1,320,1,128]{3,1,2,0:T(8,128)(2,1)S(1)}, u32[]{:S(2)}, u32[]{:S(2)}) collective-permute-start(bf16[1,320,1,128]{3,1,2,0:T(8,128)(2,1)} %bitcast.35), channel_id=1, source_target_pairs={{1,0},{2,1},{3,2},{4,3},{5,4},{6,5},{7,6},{9,8},{10,9},{11,10},{12... | collective-permute-start | bytes 245768 | tf_op jit(solution)/shard_map/ppermute | solution.py:21
  195.6 27.0 %collective-permute-start.5 = (bf16[1,320,1,128]{1,2,3,0:T(2,128)(2,1)}, bf16[1,320,1,128]{1,2,3,0:T(2,128)(2,1)}, u32[]{:S(2)}, u32[]{:S(2)}) collective-permute-start(bf16[1,320,1,128]{1,2,3,0:T(2,128)(2,1)} %slice_bitcast_fusion.16), channel_id=1, source_target_pairs={{1,0},{2,1},{3,2},{4,3},{5,4},{6,5},{7,6},{9,8},{10,9},{11,10},{12... | collective-permute-start | bytes 245768 | tf_op jit(solution)/shard_map/ppermute | solution.py:21
  197.6 23.8 %collective-permute-start.4 = (bf16[1,320,1,128]{1,3,0,2:T(8,128)(2,1)}, bf16[1,320,1,128]{1,3,0,2:T(8,128)(2,1)}, u32[]{:S(2)}, u32[]{:S(2)}) collective-permute-start(bf16[1,320,1,128]{1,3,0,2:T(8,128)(2,1)} %slice_bitcast_fusion.18), channel_id=1, source_target_pairs={{0,1},{1,2},{2,3},{3,4},{4,5},{5,6},{6,7},{8,9},{9,10},{10,11},{11... | collective-permute-start | bytes 245768 | tf_op jit(solution)/shard_map/ppermute | solution.py:20
  208.4 47.6 %collective-permute-start.10 = (f32[1,320,1,128]{1,2,3,0:T(1,128)}, f32[1,320,1,128]{1,2,3,0:T(1,128)}, u32[]{:S(2)}, u32[]{:S(2)}) collective-permute-start(f32[1,320,1,128]{1,2,3,0:T(1,128)} %slice_bitcast_fusion.14), channel_id=1, source_target_pairs={{0,1},{1,2},{2,3},{3,4},{4,5},{5,6},{6,7},{8,9},{9,10},{10,11},{11... | collective-permute-start | bytes 491528 | tf_op jit(solution)/shard_map/ppermute | solution.py:29
  215.0 5.8 copy-start.24
  215.0 46.9 %collective-permute-start.11 = (f32[1,320,1,128]{1,2,3,0:T(1,128)}, f32[1,320,1,128]{1,2,3,0:T(1,128)}, u32[]{:S(2)}, u32[]{:S(2)}) collective-permute-start(f32[1,320,1,128]{1,2,3,0:T(1,128)} %slice_bitcast_fusion.13), channel_id=1, source_target_pairs={{1,0},{2,1},{3,2},{4,3},{5,4},{6,5},{7,6},{9,8},{10,9},{11,10},{12... | collective-permute-start | bytes 491528 | tf_op jit(solution)/shard_map/ppermute | solution.py:29
  216.3 4.5 copy-start.26
  221.4 3.1 copy-start.35
  225.7 2.6 copy-start.12
  228.3 27.7 %copy-start.17 = (f32[1,8,17,320]{3,0,2,1:T(1,128)S(1)}, f32[1,8,17,320]{3,0,2,1:T(1,128)}, u32[]{:S(2)}) copy-start(f32[1,8,17,320]{3,0,2,1:T(1,128)} %copy.242) | copy-start | bytes 522244
  253.3 12.7 %collective-permute-start.8 = (bf16[1,640,1,128]{3,1,2,0:T(8,128)(2,1)}, bf16[1,640,1,128]{3,1,2,0:T(8,128)(2,1)S(1)}, u32[]{:S(2)}, u32[]{:S(2)}) collective-permute-start(bf16[1,640,1,128]{3,1,2,0:T(8,128)(2,1)} %get-tuple-element.145), channel_id=1, source_target_pairs={{0,1},{1,2},{2,3},{3,4},{4,5},{5,6},{6,7},{8,9},{9,10},{10,11},{11... | collective-permute-start | bytes 491528 | tf_op jit(solution)/shard_map/ppermute | solution.py:20
  254.6 11.4 %collective-permute-start.9 = (bf16[1,640,1,128]{3,1,2,0:T(8,128)(2,1)}, bf16[1,640,1,128]{3,1,2,0:T(8,128)(2,1)}, u32[]{:S(2)}, u32[]{:S(2)}) collective-permute-start(bf16[1,640,1,128]{3,1,2,0:T(8,128)(2,1)} %get-tuple-element.146), channel_id=1, source_target_pairs={{1,0},{2,1},{3,2},{4,3},{5,4},{6,5},{7,6},{9,8},{10,9},{11,10},{12... | collective-permute-start | bytes 491528 | tf_op jit(solution)/shard_map/ppermute | solution.py:21
  272.8 2.7 copy-start.2
  326.0 7.6 collective-permute-start.12
  328.8 10.8 %copy-start.15 = (f32[1,640,2,128]{3,1,2,0:T(8,128)S(1)}, f32[1,640,2,128]{3,1,2,0:T(8,128)}, u32[]{:S(2)}) copy-start(f32[1,640,2,128]{3,1,2,0:T(8,128)} %get-tuple-element.140) | copy-start | bytes 1966084
  332.3 7.2 collective-permute-start.13
  369.2 3.0 copy-start.39
  375.9 3.4 copy-start.25
  375.9 3.7 copy-start.9
  375.9 3.7 copy-start.10
  376.3 13.4 %collective-permute-start.14 = (f32[1,320,1,128]{1,2,3,0:T(1,128)S(1)}, f32[1,320,1,128]{1,2,3,0:T(1,128)S(1)}, u32[]{:S(2)}, u32[]{:S(2)}) collective-permute-start(f32[1,320,1,128]{1,2,3,0:T(1,128)S(1)} %slice_bitcast_fusion.11), channel_id=1, source_target_pairs={{0,1},{1,2},{2,3},{3,4},{4,5},{5,6},{6,7},{8,9},{9,10},{10,11},{11... | collective-permute-start | bytes 491528 | tf_op jit(solution)/shard_map/ppermute | solution.py:29
  381.4 7.3 copy-start.4
  386.9 11.4 %copy-start.11 = (f32[2,8,17,320]{3,0,2,1:T(2,128)S(1)}, f32[2,8,17,320]{3,0,2,1:T(2,128)}, u32[]{:S(2)}) copy-start(f32[2,8,17,320]{3,0,2,1:T(2,128)} %copy.271) | copy-start | bytes 1044484
  387.1 8.1 collective-permute-start.15
  389.9 32.0 %copy-start.33 = (f32[320]{0:T(512)S(1)}, f32[320]{0:T(512)}, u32[]{:S(2)}) copy-start(f32[320]{0:T(512)} %copy-done.32) | copy-start | bytes 3844
  432.5 429.8 %copy-start.1 = (bf16[320,3,3,320]{3,0,2,1:T(8,128)(2,1)S(1)}, bf16[320,3,3,320]{3,0,2,1:T(8,128)(2,1)}, u32[]{:S(2)}) copy-start(bf16[320,3,3,320]{3,0,2,1:T(8,128)(2,1)} %param.38) | copy-start | bytes 5529604
  432.5 426.5 %all-reduce.19.cloned.1.call-start = ((), (), s32[]{:S(2)}) async-start(), calls=%async_computation.5 | async-start | bytes 737280 | tf_op jit(solution)/shard_map/psum | solution.py:225
  (14 other events, 15.6 us)
Sparse Core Ops, SparseCore 0:
  10.6 58.0 all-gather.6
  71.3 54.9 all-gather.12
  129.0 55.0 all-gather.8
  186.5 60.2 all-gather.10
  432.6 337.0 all-reduce.16
  773.1 85.8 all-reduce.18
where the time goes:
time: 879 us; the launch traced here: 869 us
  waiting for transfers between devices  393 us (45%)
  blocking collectives  277 us (32%)
  local copies, waits for them, and re-layouts  76.4 us (9%)
  matrix products  46.1 us (5%)
  starting transfers between devices  33.6 us (4%)
  other arithmetic  25.6 us (3%)
  between operations  17.4 us (2%)
    unnamed x7, waiting for transfers between devices  337 us
    psum x4, blocking collectives, group_norm(): lax.psum((jnp.sum(grouped, axis=(2, 3, 4)), jnp.sum(grouped * grouped, ax...  85.1 us
    psum x3, blocking collectives, norm_back(): lax.psum((jnp.sum(grouped, axis=(2, 3, 4)), jnp.sum(grouped * normed_grou...  61.5 us
    all_gather x1, blocking collectives, per_device(): lax.all_gather(dec_shortcut, 'dp', axis=0, tiled=True)  49.5 us
    psum x1, waiting for transfers between devices, per_device(): lax.psum((owned[0], owned[1], owned[2]), 'rows')  48.1 us
    all_gather x1, blocking collectives, per_device(): lax.all_gather(zero_conv, 'dp', axis=0, tiled=True)  43.7 us
    psum x1, blocking collectives, per_device(): lax.psum((owned[0], owned[1], owned[2]), 'rows')  37.2 us
    unnamed x105, local copies, waits for them, and re-layouts  24.9 us
  transfers between devices with their start and end apart: 22, of which 4 were waited for; matrix products, arithmetic and copies ran while one was open for 10% of the time, Pallas kernels for 0%

commit v1 on v0

--- a/solution.py
+++ b/solution.py
@@ -167,7 +167,9 @@
         lax.all_gather(ctl_conv_two, "dp", axis=0, tiled=True),
         lax.all_gather(dec_conv_one, "dp", axis=0, tiled=True),
         lax.all_gather(dec_conv_two, "dp", axis=0, tiled=True),
-        lax.all_gather(dec_shortcut, "dp", axis=0, tiled=True),
+        jnp.concatenate(
+            lax.all_to_all(jnp.stack([dec_shortcut] * lax.axis_size("dp")), "dp", 0, 0), axis=0
+        ),
         lax.all_gather(zero_conv, "dp", axis=0, tiled=True),
     )
     half_width = C // 2

time: 879 us -> 872 us (level)
  blocking collectives: 277 us -> 233 us
  local copies, waits for them, and re-layouts: 76.4 us -> 95.8 us
  starting transfers between devices: 33.6 us -> 48.8 us
    all_gather x1 -> x0, blocking collectives: 49.5 us -> none  [per_device(): lax.all_gather(dec_shortcut, 'dp', axis=0, tiled=True)]
    all_to_all x0 -> x1, starting transfers between devices: none -> 10.8 us  [per_device(): lax.all_to_all(jnp.stack([dec_shortcut] * lax.axis_size('dp')), 'dp', 0, 0)]
    unnamed x105 -> x112, local copies, waits for them, and re-layouts: 24.9 us -> 33.3 us
  transfers between devices with their start and end apart: 22 -> 23, of which waited for: 4 -> 5; matrix products, arithmetic and copies ran while one was open for 10% -> 12% of each run, Pallas kernels for 0% -> 0%
where the time goes in v1:
time: 872 us; the launch traced here: 862 us
  waiting for transfers between devices  398 us (46%)
  blocking collectives  233 us (27%)
  local copies, waits for them, and re-layouts  95.8 us (11%)
  starting transfers between devices  48.8 us (6%)
  matrix products  45 us (5%)
  other arithmetic  24 us (3%)
  between operations  17.3 us (2%)
    unnamed x7, waiting for transfers between devices  339 us
    psum x4, blocking collectives, group_norm(): lax.psum((jnp.sum(grouped, axis=(2, 3, 4)), jnp.sum(grouped * grouped, ax...  83.7 us
    psum x3, blocking collectives, norm_back(): lax.psum((jnp.sum(grouped, axis=(2, 3, 4)), jnp.sum(grouped * normed_grou...  60 us
    all_gather x1, blocking collectives, per_device(): lax.all_gather(zero_conv, 'dp', axis=0, tiled=True)  52 us
    psum x1, waiting for transfers between devices, per_device(): lax.psum((owned[0], owned[1], owned[2]), 'rows')  48.1 us
    psum x1, blocking collectives, per_device(): lax.psum((owned[0], owned[1], owned[2]), 'rows')  37.2 us
    unnamed x112, local copies, waits for them, and re-layouts  33.3 us
    conv_general_dilated x8, matrix products, conv_rows(): lax.conv_general_dilated(padded, weight, (1, 1), ((0, 0), (1, 1)), dimens...  22.8 us
  transfers between devices with their start and end apart: 23, of which 5 were waited for; matrix products, arithmetic and copies ran while one was open for 12% of the time, Pallas kernels for 0%

profile of v1, /device:TPU:8, one launch (start us, length us, event | category | flops | bytes accessed | tf_op | source)
XLA Modules:
  0.0 861.9 jit_solution(1293333744009754316)
XLA Ops:
  11.6 20.1 %all-reduce.12 = (f32[1,32]{1,0:T(1,128)S(1)}, f32[1,32]{1,0:T(1,128)S(1)}, f32[1,32]{1,0:T(1,128)S(1)}, f32[1,32]{1,0:T(1,128)S(1)}) all-reduce(f32[1,32]{1,0:T(1,128)S(1)} %bitcast.481, f32[1,32]{1,0:T(1,128)S(1)} %bitcast.476, f32[1,32]{1,0:T(1,128)S(1)} %bitcast.479, ...), channel_id=1, replica_groups=mesh['dp'=32,'rows'=8] {'rows'}, use_global_device_ids=true, to_apply=%region_5.6 | all-reduce | flops 128 | bytes 1024 | tf_op jit(solution)/shard_map/psum | solution.py:65
  33.0 1.9 collective-permute-start
  39.0 5.2 collective-permute-start.2
  46.4 10.8 %all-to-all-start = ((bf16[32,10,640]{2,1,0:T(8,128)(2,1)}), bf16[32,10,640]{2,1,0:T(8,128)(2,1)S(1)}, u32[]{:S(2)}, u32[]{:S(2)}) async-start(bf16[32,10,640]{2,1,0:T(8,128)(2,1)} %stack.131), calls=%async_computation | async-start | bytes 1310720 | tf_op jit(solution)/shard_map/all_to_all | solution.py:171
  60.9 52.0 %all-gather = bf16[32,10,320]{2,1,0:T(8,128)(2,1)S(1)} all-gather(bf16[1,10,320]{2,1,0:T(8,128)(2,1)S(1)} %bitcast.473), channel_id=1, replica_groups=mesh['dp'=32,'rows'=8] {'dp'}, dimensions={0}, use_global_device_ids=true | all-gather | bytes 211200 | tf_op jit(solution)/shard_map/all_gather | solution.py:173
  122.2 1.7 pad_maximum_fusion.2
  123.9 1.9 copy.296
  128.4 1.8 maximum_bitcast_fusion.8
  130.2 2.0 copy.297
  135.7 3.2 fusion.27
  139.0 2.6 select_reduce_fusion.3
  143.8 20.5 %all-reduce.11 = (f32[1,32]{1,0:T(1,128)S(1)}, f32[1,32]{1,0:T(1,128)S(1)}, f32[1,32]{1,0:T(1,128)S(1)}, f32[1,32]{1,0:T(1,128)S(1)}) all-reduce(f32[1,32]{1,0:T(1,128)S(1)} %bitcast.480, f32[1,32]{1,0:T(1,128)S(1)} %bitcast.482, f32[1,32]{1,0:T(1,128)S(1)} %bitcast.478, ...), channel_id=1, replica_groups=mesh['dp'=32,'rows'=8] {'rows'}, use_global_device_ids=true, to_apply=%region_8.9 | all-reduce | flops 128 | bytes 1024 | tf_op jit(solution)/shard_map/psum | solution.py:65
  173.4 6.0 collective-permute-start.4
  179.4 3.7 fusion.14
  184.2 4.0 collective-permute-start.10
  194.0 3.0 fusion.20
  198.7 1.7 maximum_bitcast_fusion.7
  203.0 1.9 copy.286
  207.0 21.8 %all-reduce.10 = (f32[1,32]{1,0:T(1,128)S(1)}, f32[1,32]{1,0:T(1,128)S(1)}) all-reduce(f32[1,32]{1,0:T(1,128)S(1)} %bitcast.484, f32[1,32]{1,0:T(1,128)S(1)} %bitcast.489), channel_id=1, replica_groups=mesh['dp'=32,'rows'=8] {'rows'}, use_global_device_ids=true, to_apply=%region_26.27 | all-reduce | flops 64 | bytes 512 | tf_op jit(solution)/shard_map/psum | solution.py:65
  229.2 2.1 multiply_convert_fusion
  232.0 4.6 collective-permute-start.8
  238.1 1.8 fusion.131
  239.9 4.0 scatter-add.20
  245.1 2.8 scatter-add.21
  248.0 2.0 maximum_bitcast_fusion.6
  250.0 2.1 copy.299
  254.5 2.9 all-gather.10.cloned.1.call-done
  257.4 3.0 copy.236
  260.5 1.9 select_reduce_fusion.1
  262.8 21.3 %all-reduce.9 = (f32[1,32]{1,0:T(1,128)S(1)}, f32[1,32]{1,0:T(1,128)S(1)}) all-reduce(f32[1,32]{1,0:T(1,128)S(1)} %bitcast.486, f32[1,32]{1,0:T(1,128)S(1)} %bitcast.490), channel_id=1, replica_groups=mesh['dp'=32,'rows'=8] {'rows'}, use_global_device_ids=true, to_apply=%region_32.33 | all-reduce | flops 64 | bytes 512 | tf_op jit(solution)/shard_map/psum | solution.py:65
  286.0 18.0 %all-reduce.8 = (f32[1,32]{1,0:T(1,128)S(1)}, f32[1,32]{1,0:T(1,128)S(1)}) all-reduce(f32[1,32]{1,0:T(1,128)S(1)} %bitcast.491, f32[1,32]{1,0:T(1,128)S(1)} %bitcast.485), channel_id=1, replica_groups=mesh['dp'=32,'rows'=8] {'rows'}, use_global_device_ids=true, to_apply=%region_41.42 | all-reduce | flops 64 | bytes 512 | tf_op jit(solution)/shard_map/psum | solution.py:84
  305.1 3.5 fusion.17
  311.5 2.6 collective-permute-start.12
  316.9 1.7 copy.292
  320.5 1.7 copy.294
  324.5 5.1 collective-permute-done.13
  331.0 19.9 %all-reduce.7 = (f32[1,16]{1,0:T(1,128)S(1)}, f32[1,16]{1,0:T(1,128)S(1)}) all-reduce(f32[1,16]{1,0:T(1,128)S(1)} %bitcast.492, f32[1,16]{1,0:T(1,128)S(1)} %bitcast.487), channel_id=1, replica_groups=mesh['dp'=32,'rows'=8] {'rows'}, use_global_device_ids=true, to_apply=%region_47.48 | all-reduce | flops 32 | bytes 256 | tf_op jit(solution)/shard_map/psum | solution.py:84
  351.3 1.7 fusion.35
  362.6 3.7 fusion.11
  371.9 5.5 copy.283
  380.5 2.8 scatter-add.26
  383.3 2.5 collective-permute-done.15
  386.1 2.8 scatter-add.29
  389.7 22.2 %all-reduce.6 = (f32[1,32]{1,0:T(1,128)S(1)}, f32[1,32]{1,0:T(1,128)S(1)}) all-reduce(f32[1,32]{1,0:T(1,128)S(1)} %bitcast.488, f32[1,32]{1,0:T(1,128)S(1)} %bitcast.483), channel_id=1, replica_groups=mesh['dp'=32,'rows'=8] {'rows'}, use_global_device_ids=true, to_apply=%region_53.54 | all-reduce | flops 64 | bytes 512 | tf_op jit(solution)/shard_map/psum | solution.py:84
  418.1 5.5 copy.282
  425.6 336.7 %all-reduce.17.cloned.1.call-done = (f32[320,3,3,320]{3,2,1,0:T(4,128)}, f32[320,3,3,320]{3,2,1,0:T(4,128)}, f32[320,320]{1,0:T(8,128)}) async-done(((f32[320,3,3,320]{3,2,1,0:T(4,128)}, f32[320,3,3,320]{3,2,1,0:T(4,128)}, f32[320,320]{1,0:T(8,128)}), (f32[320,3,3,320]{3,2,1,0:T(4,128)}, f32[320,3,3,320]{3,2,1,0:T(4,128)}, f32[320,320]{1,0:T(8,128)})) %all-reduce.17.cloned.1.call-update) | async-done | bytes 7782416
  766.3 37.2 %psum.167 = f32[10,320]{1,0:T(8,128)} all-reduce(f32[10,320]{1,0:T(8,128)S(1)} %constant_dynamic-slice_fusion), channel_id=1, replica_groups=mesh['dp'=32,'rows'=8] {'rows'}, use_global_device_ids=true, to_apply=%region_59.60 | all-reduce | flops 3200 | bytes 25600 | tf_op jit(solution)/shard_map/psum | solution.py:227
  803.5 48.1 %all-reduce.19.cloned.1.call-done = (f32[10,3,3,320]{3,2,1,0:T(4,128)}, f32[10,3,3,320]{3,2,1,0:T(4,128)}) async-done(((f32[10,3,3,320]{3,2,1,0:T(4,128)}, f32[10,3,3,320]{3,2,1,0:T(4,128)}), (f32[10,3,3,320]{3,2,1,0:T(4,128)}, f32[10,3,3,320]{3,2,1,0:T(4,128)})) %all-reduce.19.cloned.1.call-update) | async-done | bytes 230416 | tf_op jit(solution)/shard_map/psum | solution.py:227
  (381 shorter events, 109.1 us)
Async XLA Ops:
  7.2 131.8 %copy-start = (bf16[320,3,3,320]{3,0,2,1:T(8,128)(2,1)S(1)}, bf16[320,3,3,320]{3,0,2,1:T(8,128)(2,1)}, u32[]{:S(2)}) copy-start(bf16[320,3,3,320]{3,0,2,1:T(8,128)(2,1)} %param.38) | copy-start | bytes 5529604
  7.2 38.3 %copy-start.37 = (bf16[10,640]{1,0:T(8,128)(2,1)S(1)}, bf16[10,640]{1,0:T(8,128)(2,1)}, u32[]{:S(2)}) copy-start(bf16[10,640]{1,0:T(8,128)(2,1)} %param.44) | copy-start | bytes 38404
  7.2 128.5 %all-gather.6.cloned.1.call-start = ((), (), s32[]{:S(2)}) async-start(), calls=%async_computation.1 | async-start | bytes 3041280 | tf_op jit(solution)/shard_map/all_gather | solution.py:166
  7.9 171.4 %all-gather.12.cloned.1.call-start = ((), (), s32[]{:S(2)}) async-start(), calls=%async_computation.4 | async-start | bytes 3041280 | tf_op jit(solution)/shard_map/all_gather | solution.py:169
  8.7 185.3 %all-gather.8.cloned.1.call-start = ((), (), s32[]{:S(2)}) async-start(), calls=%async_computation.2 | async-start | bytes 3041280 | tf_op jit(solution)/shard_map/all_gather | solution.py:167
  10.7 49.3 %copy-start.3 = (bf16[1,320,2,128]{3,1,2,0:T(8,128)(2,1)}, bf16[1,320,2,128]{3,1,2,0:T(8,128)(2,1)S(1)}, u32[]{:S(2)}) copy-start(bf16[1,320,2,128]{3,1,2,0:T(8,128)(2,1)S(1)} %get-tuple-element.159) | copy-start | bytes 491524
  32.0 28.0 %copy-start.34 = (bf16[1,320,2,128]{3,2,1,0:T(2,128)(2,1)S(1)}, bf16[1,320,2,128]{3,2,1,0:T(2,128)(2,1)}, u32[]{:S(2)}) copy-start(bf16[1,320,2,128]{3,2,1,0:T(2,128)(2,1)} %param.32) | copy-start | bytes 491524
  32.3 28.7 %copy-start.38 = (bf16[10,320]{1,0:T(8,128)(2,1)S(1)}, bf16[10,320]{1,0:T(8,128)(2,1)}, u32[]{:S(2)}) copy-start(bf16[10,320]{1,0:T(8,128)(2,1)} %param.45) | copy-start | bytes 19204
  33.0 89.2 %collective-permute-start = (bf16[1,320,1,128]{3,1,2,0:T(8,128)(2,1)}, bf16[1,320,1,128]{3,1,2,0:T(8,128)(2,1)}, u32[]{:S(2)}, u32[]{:S(2)}) collective-permute-start(bf16[1,320,1,128]{3,1,2,0:T(8,128)(2,1)} %get-tuple-element.153), channel_id=1, source_target_pairs={{0,1},{1,2},{2,3},{3,4},{4,5},{5,6},{6,7},{8,9},{9,10},{10,11},{11... | collective-permute-start | bytes 245768 | tf_op jit(solution)/shard_map/ppermute | solution.py:20
  34.9 87.3 %collective-permute-start.1 = (bf16[1,320,1,128]{3,1,2,0:T(8,128)(2,1)}, bf16[1,320,1,128]{3,1,2,0:T(8,128)(2,1)S(1)}, u32[]{:S(2)}, u32[]{:S(2)}) collective-permute-start(bf16[1,320,1,128]{3,1,2,0:T(8,128)(2,1)} %get-tuple-element.154), channel_id=1, source_target_pairs={{1,0},{2,1},{3,2},{4,3},{5,4},{6,5},{7,6},{9,8},{10,9},{11,10},{12... | collective-permute-start | bytes 245768 | tf_op jit(solution)/shard_map/ppermute | solution.py:21
  39.0 89.4 %collective-permute-start.2 = (bf16[1,320,1,128]{3,1,2,0:T(8,128)(2,1)}, bf16[1,320,1,128]{3,1,2,0:T(8,128)(2,1)}, u32[]{:S(2)}, u32[]{:S(2)}) collective-permute-start(bf16[1,320,1,128]{3,1,2,0:T(8,128)(2,1)} %get-tuple-element.155), channel_id=1, source_target_pairs={{0,1},{1,2},{2,3},{3,4},{4,5},{5,6},{6,7},{8,9},{9,10},{10,11},{11... | collective-permute-start | bytes 245768 | tf_op jit(solution)/shard_map/ppermute | solution.py:20
  44.2 84.3 %collective-permute-start.3 = (bf16[1,320,1,128]{3,1,2,0:T(8,128)(2,1)}, bf16[1,320,1,128]{3,1,2,0:T(8,128)(2,1)}, u32[]{:S(2)}, u32[]{:S(2)}) collective-permute-start(bf16[1,320,1,128]{3,1,2,0:T(8,128)(2,1)} %get-tuple-element.156), channel_id=1, source_target_pairs={{1,0},{2,1},{3,2},{4,3},{5,4},{6,5},{7,6},{9,8},{10,9},{11,10},{12... | collective-permute-start | bytes 245768 | tf_op jit(solution)/shard_map/ppermute | solution.py:21
  46.4 88.5 %all-to-all-start = ((bf16[32,10,640]{2,1,0:T(8,128)(2,1)}), bf16[32,10,640]{2,1,0:T(8,128)(2,1)S(1)}, u32[]{:S(2)}, u32[]{:S(2)}) async-start(bf16[32,10,640]{2,1,0:T(8,128)(2,1)} %stack.131), calls=%async_computation | async-start | bytes 1310720 | tf_op jit(solution)/shard_map/all_to_all | solution.py:171
  57.1 200.3 %all-gather.10.cloned.1.call-start = ((), (), s32[]{:S(2)}) async-start(), calls=%async_computation.3 | async-start | bytes 5068800 | tf_op jit(solution)/shard_map/all_gather | solution.py:168
  57.7 704.5 %all-reduce.17.cloned.1.call-start = ((), (), s32[]{:S(2)}) async-start(), calls=%async_computation.5 | async-start | bytes 24576000
  117.4 4.5 copy-start.20
  122.2 10.0 %copy-start.28 = (bf16[1,320,1,128]{3,1,2,0:T(8,128)(2,1)}, bf16[1,320,1,128]{3,1,2,0:T(8,128)(2,1)S(1)}, u32[]{:S(2)}) copy-start(bf16[1,320,1,128]{3,1,2,0:T(8,128)(2,1)S(1)} %collective-permute-done.1) | copy-start | bytes 245764
  127.8 7.9 copy-start.41
  135.7 3.2 copy-start.35
  135.7 3.2 copy-start.42
  165.8 4.2 copy-start.27
  166.4 25.1 %collective-permute-start.6 = (bf16[1,320,1,128]{3,1,2,0:T(8,128)(2,1)S(1)}, bf16[1,320,1,128]{3,1,2,0:T(8,128)(2,1)S(1)}, u32[]{:S(2)}, u32[]{:S(2)}) collective-permute-start(bf16[1,320,1,128]{3,1,2,0:T(8,128)(2,1)S(1)} %bitcast.471), channel_id=1, source_target_pairs={{0,1},{1,2},{2,3},{3,4},{4,5},{5,6},{6,7},{8,9},{9,10},{10,11},{11... | collective-permute-start | bytes 245768 | tf_op jit(solution)/shard_map/ppermute | solution.py:20
  167.8 11.6 %copy-start.33 = (bf16[320,2,1,8,17]{0,3,4,1,2:T(8,128)(2,1)S(1)}, bf16[320,2,1,8,17]{0,3,4,1,2:T(8,128)(2,1)}, u32[]{:S(2)}) copy-start(bf16[320,2,1,8,17]{0,3,4,1,2:T(8,128)(2,1)} %copy-done.32) | copy-start | bytes 522244
  167.8 11.6 %copy-start.36 = (bf16[320,2,1,7,2]{0,3,4,1,2:T(8,128)(2,1)S(1)}, bf16[320,2,1,7,2]{0,3,4,1,2:T(8,128)(2,1)}, u32[]{:S(2)}) copy-start(bf16[320,2,1,7,2]{0,3,4,1,2:T(8,128)(2,1)} %slice.424) | copy-start | bytes 53764
  167.8 11.6 %copy-start.43 = (pred[8,17]{0,1:T(8,128)(4,1)S(1)}, pred[8,17]{0,1:T(8,128)(4,1)}, u32[]{:S(2)}) copy-start(pred[8,17]{0,1:T(8,128)(4,1)} %constant.237) | copy-start | bytes 412
  168.0 24.8 %collective-permute-start.7 = (bf16[1,320,1,128]{3,1,2,0:T(8,128)(2,1)S(1)}, bf16[1,320,1,128]{3,1,2,0:T(8,128)(2,1)S(1)}, u32[]{:S(2)}, u32[]{:S(2)}) collective-permute-start(bf16[1,320,1,128]{3,1,2,0:T(8,128)(2,1)S(1)} %bitcast.472), channel_id=1, source_target_pairs={{1,0},{2,1},{3,2},{4,3},{5,4},{6,5},{7,6},{9,8},{10,9},{11,10},{12... | collective-permute-start | bytes 245768 | tf_op jit(solution)/shard_map/ppermute | solution.py:21
  171.3 27.4 %collective-permute-start.5 = (bf16[1,320,1,128]{1,2,3,0:T(2,128)(2,1)}, bf16[1,320,1,128]{1,2,3,0:T(2,128)(2,1)}, u32[]{:S(2)}, u32[]{:S(2)}) collective-permute-start(bf16[1,320,1,128]{1,2,3,0:T(2,128)(2,1)} %slice_bitcast_fusion.16), channel_id=1, source_target_pairs={{1,0},{2,1},{3,2},{4,3},{5,4},{6,5},{7,6},{9,8},{10,9},{11,10},{12... | collective-permute-start | bytes 245768 | tf_op jit(solution)/shard_map/ppermute | solution.py:21
  173.4 24.2 %collective-permute-start.4 = (bf16[1,320,1,128]{1,3,0,2:T(8,128)(2,1)}, bf16[1,320,1,128]{1,3,0,2:T(8,128)(2,1)}, u32[]{:S(2)}, u32[]{:S(2)}) collective-permute-start(bf16[1,320,1,128]{1,3,0,2:T(8,128)(2,1)} %slice_bitcast_fusion.18), channel_id=1, source_target_pairs={{0,1},{1,2},{2,3},{3,4},{4,5},{5,6},{6,7},{8,9},{9,10},{10,11},{11... | collective-permute-start | bytes 245768 | tf_op jit(solution)/shard_map/ppermute | solution.py:20
  184.2 53.9 %collective-permute-start.10 = (f32[1,320,1,128]{1,2,3,0:T(1,128)}, f32[1,320,1,128]{1,2,3,0:T(1,128)}, u32[]{:S(2)}, u32[]{:S(2)}) collective-permute-start(f32[1,320,1,128]{1,2,3,0:T(1,128)} %slice_bitcast_fusion.14), channel_id=1, source_target_pairs={{0,1},{1,2},{2,3},{3,4},{4,5},{5,6},{6,7},{8,9},{9,10},{10,11},{11... | collective-permute-start | bytes 491528 | tf_op jit(solution)/shard_map/ppermute | solution.py:29
  191.5 52.4 %collective-permute-start.11 = (f32[1,320,1,128]{1,2,3,0:T(1,128)}, f32[1,320,1,128]{1,2,3,0:T(1,128)}, u32[]{:S(2)}, u32[]{:S(2)}) collective-permute-start(f32[1,320,1,128]{1,2,3,0:T(1,128)} %slice_bitcast_fusion.13), channel_id=1, source_target_pairs={{1,0},{2,1},{3,2},{4,3},{5,4},{6,5},{7,6},{9,8},{10,9},{11,10},{12... | collective-permute-start | bytes 491528 | tf_op jit(solution)/shard_map/ppermute | solution.py:29
  201.9 4.4 copy-start.15
  203.0 35.1 %copy-start.21 = (f32[1,8,17,320]{3,0,2,1:T(1,128)S(1)}, f32[1,8,17,320]{3,0,2,1:T(1,128)}, u32[]{:S(2)}) copy-start(f32[1,8,17,320]{3,0,2,1:T(1,128)} %copy.242) | copy-start | bytes 522244
  232.0 16.0 %collective-permute-start.8 = (bf16[1,640,1,128]{3,1,2,0:T(8,128)(2,1)}, bf16[1,640,1,128]{3,1,2,0:T(8,128)(2,1)}, u32[]{:S(2)}, u32[]{:S(2)}) collective-permute-start(bf16[1,640,1,128]{3,1,2,0:T(8,128)(2,1)} %get-tuple-element.145), channel_id=1, source_target_pairs={{0,1},{1,2},{2,3},{3,4},{4,5},{5,6},{6,7},{8,9},{9,10},{10,11},{11... | collective-permute-start | bytes 491528 | tf_op jit(solution)/shard_map/ppermute | solution.py:20
  236.6 11.4 %collective-permute-start.9 = (bf16[1,640,1,128]{3,1,2,0:T(8,128)(2,1)}, bf16[1,640,1,128]{3,1,2,0:T(8,128)(2,1)}, u32[]{:S(2)}, u32[]{:S(2)}) collective-permute-start(bf16[1,640,1,128]{3,1,2,0:T(8,128)(2,1)} %get-tuple-element.146), channel_id=1, source_target_pairs={{1,0},{2,1},{3,2},{4,3},{5,4},{6,5},{7,6},{9,8},{10,9},{11,10},{12... | collective-permute-start | bytes 491528 | tf_op jit(solution)/shard_map/ppermute | solution.py:21
  310.4 4.0 slice-start
  311.5 12.0 %collective-permute-start.12 = (f32[1,320,1,128]{3,1,2,0:T(8,128)}, f32[1,320,1,128]{3,1,2,0:T(8,128)}, u32[]{:S(2)}, u32[]{:S(2)}) collective-permute-start(f32[1,320,1,128]{3,1,2,0:T(8,128)} %bitcast.86), channel_id=1, source_target_pairs={{0,1},{1,2},{2,3},{3,4},{4,5},{5,6},{6,7},{8,9},{9,10},{10,11},{11... | collective-permute-start | bytes 491528 | tf_op jit(solution)/shard_map/ppermute | solution.py:29
  314.9 14.8 %copy-start.17 = (f32[1,640,2,128]{3,1,2,0:T(8,128)S(1)}, f32[1,640,2,128]{3,1,2,0:T(8,128)}, u32[]{:S(2)}) copy-start(f32[1,640,2,128]{3,1,2,0:T(8,128)} %get-tuple-element.140) | copy-start | bytes 1966084
  322.2 7.5 collective-permute-start.13
  352.9 5.9 copy-start.22
  366.3 3.6 copy-start.11
  366.3 3.6 copy-start.12
  366.7 13.6 %collective-permute-start.14 = (f32[1,320,1,128]{1,2,3,0:T(1,128)S(1)}, f32[1,320,1,128]{1,2,3,0:T(1,128)S(1)}, u32[]{:S(2)}, u32[]{:S(2)}) collective-permute-start(f32[1,320,1,128]{1,2,3,0:T(1,128)S(1)} %slice_bitcast_fusion.11), channel_id=1, source_target_pairs={{0,1},{1,2},{2,3},{3,4},{4,5},{5,6},{6,7},{8,9},{9,10},{10,11},{11... | collective-permute-start | bytes 491528 | tf_op jit(solution)/shard_map/ppermute | solution.py:29
  371.9 7.3 copy-start.5
  371.9 7.3 copy-start.23
  377.5 11.4 %copy-start.14 = (f32[2,8,17,320]{3,0,2,1:T(2,128)S(1)}, f32[2,8,17,320]{3,0,2,1:T(2,128)}, u32[]{:S(2)}) copy-start(f32[2,8,17,320]{3,0,2,1:T(2,128)} %copy.271) | copy-start | bytes 1044484
  377.7 8.1 collective-permute-start.15
  423.7 431.1 %copy-start.1 = (bf16[320,3,3,320]{3,0,2,1:T(8,128)(2,1)S(1)}, bf16[320,3,3,320]{3,0,2,1:T(8,128)(2,1)}, u32[]{:S(2)}) copy-start(bf16[320,3,3,320]{3,0,2,1:T(8,128)(2,1)} %param.38) | copy-start | bytes 5529604
  423.7 427.9 %all-reduce.19.cloned.1.call-start = ((), (), s32[]{:S(2)}) async-start(), calls=%async_computation.6 | async-start | bytes 737280 | tf_op jit(solution)/shard_map/psum | solution.py:227
  (20 other events, 28.3 us)
Sparse Core Ops, SparseCore 0:
  10.6 60.4 all-gather.5
  73.7 62.7 all-gather.11
  139.1 53.3 all-gather.7
  194.9 62.4 all-gather.9
  423.8 338.3 all-reduce.16
  765.7 85.8 all-reduce.18
